TPU v7x, 512 devices: a whole 4x8x8 slice. The times are simulated.
512 devices in a mesh: section: 16 (over x_lo, z), dp: 32 (over x_hi, y, core).
Axes of the slice: x: 4 (x_hi: 2, x_lo: 2; x = x_hi * 2 + x_lo), y: 8, z: 8, core: 2. Of those that a mesh axis runs over, the one named last changes fastest.
Arguments:
- act_in: float32 [16, 2, 32, 15, 15, 256], P('section', None, 'dp'), may hold values from -6 to 6
- act_mid: float32 [16, 2, 32, 15, 15, 256], P('section', None, 'dp'), may hold values from 0 to 2
- relu_mask: int32 [16, 2, 32, 15, 15, 256], P('section', None, 'dp'), may hold values 0 or 1
- arriving: float32 [16, 32, 15, 15, 256], P('section', 'dp'), may hold values from -6 to 6
- loss_grad: float32 [1, 32, 15, 15, 256], P(None, 'dp'), may hold values from -6 to 6
- w_first: float32 [16, 1792, 256], P('section', 'dp'), may hold values from -0.125 to 0.125
- w_second: float32 [16, 1792, 256], P('section', 'dp'), may hold values from -0.125 to 0.125
Outputs:
- data_grad: float32 [16, 2, 32, 15, 15, 256], P('section', None, 'dp')
- first_grad: float32 [16, 1792, 256], P('section', 'dp')
- second_grad: float32 [16, 1792, 256], P('section', 'dp')
All inputs are finite; a program needn't handle non-finite values. No bound on the sum of `relu_mask` on one device may be relied on, other than what follows from the above.
Results may differ from a plain program's by a relative error of at most 0.00011.
Values sent between devices are 32-bit elements; how exact they have to be, the bound alone decides.
A program may use at most 64 MiB of HBM per device.

v0:
```python
import jax
import jax.numpy as jnp
from jax import lax
from jax.sharding import PartitionSpec as P


def shifted(shard, axis, by):
    peers = lax.axis_size(axis)
    pairs = [(i, i + by) for i in range(peers) if 0 <= i + by < peers]
    return lax.ppermute(shard, axis, pairs)


def spread_taps(values, spatial):
    widths = [(0, 0)] * 4
    widths[spatial] = (3, 3)
    padded = jnp.pad(values, widths)
    extent = values.shape[spatial]
    pieces = [
        lax.slice_in_dim(padded, offset, offset + extent, axis=spatial) for offset in range(7)
    ]
    return jnp.concatenate(pieces, axis=-1)


def fold_taps(products, spatial):
    channels = products.shape[-1] // 7
    widths = [(0, 0)] * 4
    widths[spatial] = (3, 3)
    padded = jnp.pad(products, widths)
    extent = products.shape[spatial]
    summed = jnp.zeros(products.shape[:-1] + (channels,), products.dtype)
    for offset in range(7):
        window = lax.slice_in_dim(padded, 6 - offset, 6 - offset + extent, axis=spatial)
        summed = summed + window[..., offset * channels : (offset + 1) * channels]
    return summed


def project_taps(values, weight):
    return jnp.einsum("nhwc,kc->nhwk", values, weight, precision=lax.Precision.HIGHEST)


def flat_patches(values, spatial):
    patches = spread_taps(values.reshape((-1,) + values.shape[2:]), spatial)
    return patches.reshape(-1, patches.shape[-1])


def correlate(patches, grad_rows, mean_scale):
    return jnp.einsum("rk,rc->kc", patches, grad_rows, precision=lax.Precision.HIGHEST) * mean_scale


def local(act_in, act_mid, relu_mask, arriving, loss_grad, w_first, w_second):
    tick_count = act_in.shape[1]
    channels = act_in.shape[-1]
    is_last = lax.axis_index("section") == lax.axis_size("section") - 1
    full_first, full_second = (
        lax.all_gather(w_first[0], "dp", axis=0, tiled=True),
        lax.all_gather(w_second[0], "dp", axis=0, tiled=True),
    )
    incoming = arriving[0]
    mid_grad = fold_taps(project_taps(incoming, full_second), 1)
    in_list = [incoming]
    pre_list = []
    out_list = []
    for tick_index in range(tick_count):
        if tick_index > 0:
            from_above = shifted(out_list[-1], "section", -1)
            incoming = jnp.where(is_last, loss_grad[tick_index - 1], from_above)
            in_list.append(incoming)
            mid_grad = fold_taps(project_taps(incoming, full_second), 1)
        pre_grad = mid_grad * relu_mask[0, tick_index].astype(jnp.float32)
        out_list.append(fold_taps(project_taps(pre_grad, full_first), 2))
        pre_list.append(pre_grad)
    data_grad = jnp.stack(out_list, axis=0)[None]
    mean_scale = 1.0 / (tick_count * act_in.shape[2] * lax.axis_size("dp"))
    first_patches = flat_patches(act_in[0], 2)
    second_patches = flat_patches(act_mid[0], 1)
    pre_rows = jnp.stack(pre_list, axis=0).reshape(-1, channels)
    in_rows = jnp.stack(in_list, axis=0).reshape(-1, channels)
    summed = lax.psum_scatter(
        jnp.concatenate(
            [
                correlate(first_patches, pre_rows, mean_scale),
                correlate(second_patches, in_rows, mean_scale),
            ],
            axis=1,
        ),
        "dp",
        scatter_dimension=0,
        tiled=True,
    )
    first_grad = summed[:, :channels]
    second_grad = summed[:, channels:]
    return (data_grad, first_grad[None], second_grad[None])


def solution(mesh):
    return jax.shard_map(
        local,
        mesh=mesh,
        in_specs=(
            P("section", None, "dp", None, None, None),
            P("section", None, "dp", None, None, None),
            P("section", None, "dp", None, None, None),
            P("section", "dp", None, None, None),
            P(None, "dp", None, None, None),
            P("section", "dp", None),
            P("section", "dp", None),
        ),
        out_specs=(
            P("section", None, "dp", None, None, None),
            P("section", "dp", None),
            P("section", "dp", None),
        ),
        check_vma=False,
    )
```

profile of v0, /device:TPU:16, one launch (start us, length us, event | category | flops | bytes accessed | tf_op | source)
XLA Modules:
  0.0 363.2 jit_solution(2133980787343362848)
XLA Ops:
  8.7 1.3 copy.89
  10.0 2.1 reduce.1
  12.1 2.0 copy.90
  14.1 2.1 reduce
  16.3 1.7 pad_slice_fusion.24
  18.5 1.1 copy.52
  20.4 1.1 copy.53
  22.4 1.6 copy.54
  24.0 4.0 %pad_slice_fusion.30 = (f32[2,15,15,256]{3,0,2,1:T(2,128)}, f32[2,15,15,256]{3,0,2,1:T(2,128)}, f32[2,15,15,256]{3,0,2,1:T(2,128)}, f32[2,15,15,256]{3,0,2,1:T(2...) fusion(f32[2,15,15,256]{3,0,2,1:T(2,128)} %bitcast.66), kind=kLoop, calls=%fused_computation.46 | loop fusion | bytes 3225600 | tf_op jit(solution)/shard_map/slice | solution.py:19
  29.0 1.1 copy.42
  30.9 1.1 copy.43
  32.8 0.9 concatenate.42
  33.6 1.1 copy.44
  35.6 1.1 copy.45
  39.2 1.9 constant_dynamic-update-slice_fusion.6
  49.6 1.0 fusion.39
  50.6 48.9 %all-gather.5.cloned.1.call-done = f32[1,1792,256]{2,1,0:T(8,128)} async-done(((f32[1,56,256]{2,1,0:T(8,128)}), f32[1,1792,256]{2,1,0:T(8,128)}) %all-gather.5.cloned.1.call-update) | async-done | bytes 1835024 | tf_op jit(solution)/shard_map/all_gather | solution.py:56
  99.5 3.2 convolution_bitcast_fusion.3
  102.8 81.2 %all-gather.7.cloned.1.call-done = f32[1,1792,256]{2,1,0:T(8,128)} async-done(((f32[1,56,256]{2,1,0:T(8,128)}), f32[1,1792,256]{2,1,0:T(8,128)}) %all-gather.7.cloned.1.call-update) | async-done | bytes 1835024 | tf_op jit(solution)/shard_map/all_gather | solution.py:55
  184.1 3.3 convolution_bitcast_fusion.2
  187.6 1.6 collective-permute-start
  190.9 6.8 %collective-permute-done = f32[1,15,15,256]{3,2,1,0:T(8,128)S(1)} collective-permute-done((f32[1,15,15,256]{3,2,1,0:T(8,128)S(1)}, f32[1,15,15,256]{3,2,1,0:T(8,128)S(1)}, u32[]{:S(2)}, u32[]{:S(2)}) %collective-permute-start) | collective-permute-done | bytes 230432 | tf_op jit(solution)/shard_map/ppermute | solution.py:10
  199.2 1.9 reshape.78
  201.1 2.8 convolution_bitcast_fusion.1
  204.9 5.2 %convolution_multiply_fusion = f32[1792,256]{0,1:T(8,128)S(1)} fusion(f32[450,1792]{1,0:T(8,128)} %constant_dynamic-update-slice_fusion.7, f32[450,256]{1,0:T(8,128)S(1)} %copy-done.13), kind=kOutput, calls=%fused_computation.25 | convolution fusion | flops 2477719552 | bytes 5521408 | tf_op jit(solution)/shard_map/rk,rc->kc/dot_general | solution.py:47
  210.0 5.3 %convolution_multiply_fusion.1 = f32[1792,256]{0,1:T(8,128)S(1)} fusion(f32[450,1792]{1,0:T(8,128)} %constant_dynamic-update-slice_fusion, f32[450,256]{1,0:T(8,128)S(1)} %reshape.77), kind=kOutput, calls=%fused_computation.26 | convolution fusion | flops 2477719552 | bytes 5521408 | tf_op jit(solution)/shard_map/rk,rc->kc/dot_general | solution.py:47
  215.3 2.1 pad_maximum_fusion
  217.4 5.2 %copy.58 = f32[1792,512]{1,0:T(8,128)} copy(f32[1792,512]{0,1:T(8,128)} %pad_maximum_fusion) | data formatting | bytes 7340032
  222.8 1.3 copy-done
  224.1 2.6 convolution_bitcast_fusion
  226.9 1.2 copy.55
  228.2 126.0 %reduce-scatter.4.cloned.1.call-done = f32[56,512]{1,0:T(8,128)} async-done(((f32[1792,512]{1,0:T(8,128)}), f32[56,512]{1,0:T(8,128)}) %reduce-scatter.4.cloned.1.call-update) | async-done | bytes 114704
  (94 shorter events, 25.4 us)
Async XLA Ops:
  7.2 92.3 %all-gather.5.cloned.1.call-start = ((), (), s32[]{:S(2)}) async-start(), calls=%async_computation.1 | async-start | bytes 1892352 | tf_op jit(solution)/shard_map/all_gather | solution.py:56
  7.9 176.2 %all-gather.7.cloned.1.call-start = ((), (), s32[]{:S(2)}) async-start(), calls=%async_computation.2 | async-start | bytes 1892352 | tf_op jit(solution)/shard_map/all_gather | solution.py:55
  8.6 345.5 %reduce-scatter.4.cloned.1.call-start = ((), (), s32[]{:S(2)}) async-start(), calls=%async_computation.3 | async-start | bytes 3784704
  32.8 4.7 %copy-start.14 = (f32[2,15,15,256]{3,0,2,1:T(2,128)S(1)}, f32[2,15,15,256]{3,0,2,1:T(2,128)}, u32[]{:S(2)}) copy-start(f32[2,15,15,256]{3,0,2,1:T(2,128)} %get-tuple-element.12) | copy-start | bytes 1382404
  37.5 7.0 %copy-start.6 = (f32[450,256]{1,0:T(8,128)S(1)}, f32[450,256]{1,0:T(8,128)}, u32[]{:S(2)}) copy-start(f32[450,256]{1,0:T(8,128)} %concatenate.52) | copy-start | bytes 1382404
  38.4 7.0 %copy-start.8 = (f32[450,256]{1,0:T(8,128)S(1)}, f32[450,256]{1,0:T(8,128)}, u32[]{:S(2)}) copy-start(f32[450,256]{1,0:T(8,128)} %concatenate.53) | copy-start | bytes 1382404
  39.2 7.0 %copy-start.9 = (f32[450,256]{1,0:T(8,128)S(1)}, f32[450,256]{1,0:T(8,128)}, u32[]{:S(2)}) copy-start(f32[450,256]{1,0:T(8,128)} %concatenate.40) | copy-start | bytes 1382404
  41.2 5.9 %copy-start.11 = (f32[450,256]{1,0:T(8,128)S(1)}, f32[450,256]{1,0:T(8,128)}, u32[]{:S(2)}) copy-start(f32[450,256]{1,0:T(8,128)} %concatenate.41) | copy-start | bytes 1382404
  42.0 5.9 %copy-start.10 = (f32[450,256]{1,0:T(8,128)S(1)}, f32[450,256]{1,0:T(8,128)}, u32[]{:S(2)}) copy-start(f32[450,256]{1,0:T(8,128)} %concatenate.42) | copy-start | bytes 1382404
  42.9 5.9 %copy-start.12 = (f32[450,256]{1,0:T(8,128)S(1)}, f32[450,256]{1,0:T(8,128)}, u32[]{:S(2)}) copy-start(f32[450,256]{1,0:T(8,128)} %concatenate.43) | copy-start | bytes 1382404
  43.7 5.9 %copy-start.20 = (s32[1,2,1,15,15,256]{5,2,4,3,1,0:T(1,128)S(1)}, s32[1,2,1,15,15,256]{5,2,4,3,1,0:T(1,128)}, u32[]{:S(2)}) copy-start(s32[1,2,1,15,15,256]{5,2,4,3,1,0:T(1,128)} %param.9) | copy-start | bytes 1382404
  44.6 54.9 %copy-start.16 = (f32[1,1,15,15,256]{4,1,3,2,0:T(1,128)S(1)}, f32[1,1,15,15,256]{4,1,3,2,0:T(1,128)}, u32[]{:S(2)}) copy-start(f32[1,1,15,15,256]{4,1,3,2,0:T(1,128)} %param.10) | copy-start | bytes 691204
  102.8 81.3 %copy-start.2 = (f32[1,15,15,256]{3,2,1,0:T(8,128)}, f32[1,15,15,256]{3,2,1,0:T(8,128)S(1)}, u32[]{:S(2)}) copy-start(f32[1,15,15,256]{3,2,1,0:T(8,128)S(1)} %fusion.10) | copy-start | bytes 691204
  184.1 5.1 %copy-start.5 = (f32[450,256]{1,0:T(8,128)S(1)}, f32[450,256]{1,0:T(8,128)}, u32[]{:S(2)}) copy-start(f32[450,256]{1,0:T(8,128)} %concatenate.44) | copy-start | bytes 1382404
  184.1 5.9 %copy-start.7 = (f32[450,256]{1,0:T(8,128)S(1)}, f32[450,256]{1,0:T(8,128)}, u32[]{:S(2)}) copy-start(f32[450,256]{1,0:T(8,128)} %concatenate.45) | copy-start | bytes 1382404
  184.1 13.6 %copy-start.15 = (f32[1,1,15,15,256]{4,1,3,2,0:T(1,128)S(1)}, f32[1,1,15,15,256]{4,1,3,2,0:T(1,128)}, u32[]{:S(2)}) copy-start(f32[1,1,15,15,256]{4,1,3,2,0:T(1,128)} %param.11) | copy-start | bytes 691204
  187.4 11.0 %copy-start.18 = (f32[1,1,15,15,256]{4,3,2,1,0:T(8,128)S(1)}, f32[1,1,15,15,256]{4,3,2,1,0:T(8,128)}, u32[]{:S(2)}) copy-start(f32[1,1,15,15,256]{4,3,2,1,0:T(8,128)} %copy.54) | copy-start | bytes 691204
  187.4 13.7 %copy-start.1 = (f32[1,1792,256]{2,1,0:T(8,128)S(1)}, f32[1,1792,256]{2,1,0:T(8,128)}, u32[]{:S(2)}) copy-start(f32[1,1792,256]{2,1,0:T(8,128)} %all-gather.5.cloned.1.call-done) | copy-start | bytes 5505028
  187.6 10.1 %collective-permute-start = (f32[1,15,15,256]{3,2,1,0:T(8,128)S(1)}, f32[1,15,15,256]{3,2,1,0:T(8,128)S(1)}, u32[]{:S(2)}, u32[]{:S(2)}) collective-permute-start(f32[1,15,15,256]{3,2,1,0:T(8,128)S(1)} %fusion.23), channel_id=1, source_target_pairs={{32,0},{64,32},{96,64},{128,96},{160,128},{192,160},{224,192},{256... | collective-permute-start | bytes 691208 | tf_op jit(solution)/shard_map/ppermute | solution.py:10
  197.7 0.7 copy-start.17
  201.1 2.8 copy-start.19
  201.1 3.6 %copy-start.3 = (f32[1,15,15,256]{3,2,1,0:T(8,128)S(1)}, f32[1,15,15,256]{3,2,1,0:T(8,128)}, u32[]{:S(2)}) copy-start(f32[1,15,15,256]{3,2,1,0:T(8,128)} %copy-done.2) | copy-start | bytes 691204
  203.9 1.0 copy-start.13
  204.0 0.7 copy-start.4
  222.6 1.5 copy-start
Sparse Core Ops, SparseCore 0:
  11.3 88.1 all-gather.4
  102.8 81.1 all-gather.6
  222.7 131.3 reduce-scatter.3
where the time goes:
time: 364 us; the launch traced here: 363 us
  waiting for transfers between devices  264 us (73%)
  local copies, waits for them, and re-layouts  52.7 us (14%)
  matrix products  22.3 us (6%)
  between operations  14.1 us (4%)
  other arithmetic  8.07 us (2%)
    unnamed x4, waiting for transfers between devices  127 us
    all_gather x1, waiting for transfers between devices, local(): lax.all_gather(w_first[0], 'dp', axis=0, tiled=True)  81.2 us
    all_gather x1, waiting for transfers between devices, local(): lax.all_gather(w_second[0], 'dp', axis=0, tiled=True)  48.9 us
    unnamed x63, local copies, waits for them, and re-layouts  26.9 us
    slice x14, local copies, waits for them, and re-layouts, spread_taps(): lax.slice_in_dim(padded, offset, offset + extent, axis=spatial)  12.5 us
    dot_general x4, matrix products, project_taps(): jnp.einsum('nhwc,kc->nhwk', values, weight, precision=lax.Precision.HIGHEST)  11.9 us
    dot_general x2, matrix products, correlate(): jnp.einsum('rk,rc->kc', patches, grad_rows, precision=lax.Precision.HIGHEST)  10.4 us
    concatenate x16, local copies, waits for them, and re-layouts, spread_taps(): return jnp.concatenate(pieces, axis=-1)  9.53 us
  transfers between devices with their start and end apart: 4, of which 4 were waited for; matrix products, arithmetic and copies ran while one was open for 14% of the time, Pallas kernels for 0%

commit v1 on v0

--- a/solution.py
+++ b/solution.py
@@ -2,6 +2,13 @@
 import jax.numpy as jnp
 from jax import lax
 from jax.sharding import PartitionSpec as P
+
+
+def swapped_in(x, axis, dim):
+    size = lax.axis_size(axis)
+    blocks = jnp.stack([x for _ in range(size)])
+    blocks = lax.all_to_all(blocks, axis, split_axis=0, concat_axis=0)
+    return jnp.concatenate(blocks, axis=dim)
 
 
 def shifted(shard, axis, by):
@@ -53,7 +60,7 @@
     is_last = lax.axis_index("section") == lax.axis_size("section") - 1
     full_first, full_second = (
         lax.all_gather(w_first[0], "dp", axis=0, tiled=True),
-        lax.all_gather(w_second[0], "dp", axis=0, tiled=True),
+        swapped_in(w_second[0], "dp", 0),
     )
     incoming = arriving[0]
     mid_grad = fold_taps(project_taps(incoming, full_second), 1)

time: 364 us -> 295 us (0.81)
  waiting for transfers between devices: 264 us -> 180 us
  starting transfers between devices: 1.72 us -> 11.6 us
  local copies, waits for them, and re-layouts: 52.7 us -> 59.1 us
    all_gather x1 -> x0, waiting for transfers between devices: 48.9 us -> none  [local(): lax.all_gather(w_second[0], 'dp', axis=0, tiled=True)]
    all_gather x1, waiting for transfers between devices: 81.2 us -> 46.7 us  [local(): lax.all_gather(w_first[0], 'dp', axis=0, tiled=True)]
    all_to_all x0 -> x1, starting transfers between devices: none -> 10.1 us  [swapped_in(): blocks = lax.all_to_all(blocks, axis, split_axis=0, concat_axis=0)]
    concatenate x16, local copies, waits for them, and re-layouts: 9.53 us -> 13.5 us  [spread_taps(): return jnp.concatenate(pieces, axis=-1)]
    unnamed x63 -> x71, local copies, waits for them, and re-layouts: 26.9 us -> 26 us
    unnamed x4 -> x3, waiting for transfers between devices: 127 us -> 127 us
  transfers between devices with their start and end apart: 4 -> 4, of which waited for: 4 -> 3; matrix products, arithmetic and copies ran while one was open for 14% -> 18% of each run, Pallas kernels for 0% -> 0%
where the time goes in v1:
time: 295 us; the launch traced here: 294 us
  waiting for transfers between devices  180 us (61%)
  local copies, waits for them, and re-layouts  59.1 us (20%)
  matrix products  20.9 us (7%)
  between operations  14.4 us (5%)
  starting transfers between devices  11.6 us (4%)
  other arithmetic  7.72 us (3%)
    unnamed x3, waiting for transfers between devices  127 us
    all_gather x1, waiting for transfers between devices, local(): lax.all_gather(w_first[0], 'dp', axis=0, tiled=True)  46.7 us
    unnamed x71, local copies, waits for them, and re-layouts  26 us
    slice x14, local copies, waits for them, and re-layouts, spread_taps(): lax.slice_in_dim(padded, offset, offset + extent, axis=spatial)  13.6 us
    concatenate x16, local copies, waits for them, and re-layouts, spread_taps(): return jnp.concatenate(pieces, axis=-1)  13.5 us
    dot_general x4, matrix products, project_taps(): jnp.einsum('nhwc,kc->nhwk', values, weight, precision=lax.Precision.HIGHEST)  10.5 us
    dot_general x2, matrix products, correlate(): jnp.einsum('rk,rc->kc', patches, grad_rows, precision=lax.Precision.HIGHEST)  10.4 us
    all_to_all x1, starting transfers between devices, swapped_in(): blocks = lax.all_to_all(blocks, axis, split_axis=0, concat_axis=0)  10.1 us
  transfers between devices with their start and end apart: 4, of which 3 were waited for; matrix products, arithmetic and copies ran while one was open for 18% of the time, Pallas kernels for 0%

profile of v1, /device:TPU:16, one launch (start us, length us, event | category | flops | bytes accessed | tf_op | source)
XLA Modules:
  0.0 294.0 jit_solution(2443735970570894730)
XLA Ops:
  7.2 2.2 stack.27
  9.4 10.1 %all-to-all-start = ((f32[32,56,256]{2,1,0:T(8,128)}), f32[32,56,256]{2,1,0:T(8,128)S(1)}, u32[]{:S(2)}, u32[]{:S(2)}) async-start(f32[32,56,256]{2,1,0:T(8,128)} %stack.27), calls=%async_computation | async-start | bytes 3670016 | tf_op jit(solution)/shard_map/all_to_all | solution.py:10
  20.5 1.1 reduce.1
  21.6 2.1 copy.90
  23.6 2.1 reduce
  25.8 1.8 pad_slice_fusion.24
  28.5 1.1 copy.49
  30.4 1.1 copy.50
  33.2 1.1 copy.51
  35.2 1.1 copy.52
  37.1 1.1 copy.53
  39.7 1.8 pad_slice_fusion.30
  42.5 1.1 copy.42
  44.4 1.1 copy.43
  48.1 1.1 copy.45
  52.8 1.9 constant_dynamic-update-slice_fusion.6
  55.5 1.9 constant_dynamic-update-slice_fusion.11
  65.3 1.7 convolution_bitcast_fusion.3
  67.8 46.7 %all-gather.3.cloned.1.call-done = f32[1,1792,256]{2,1,0:T(8,128)} async-done(((f32[1,56,256]{2,1,0:T(8,128)}), f32[1,1792,256]{2,1,0:T(8,128)}) %all-gather.3.cloned.1.call-update) | async-done | bytes 1835024 | tf_op jit(solution)/shard_map/all_gather | solution.py:62
  114.5 3.4 %convolution_bitcast_fusion.2 = f32[1,15,15,1792]{3,2,1,0:T(8,128)S(1)} fusion(f32[1,1792,256]{2,1,0:T(8,128)} %all-gather.3.cloned.1.call-done, f32[1,15,15,256]{3,2,1,0:T(8,128)} %fusion.8), kind=kOutput, calls=%fused_computation.29 | convolution fusion | flops 1238630400 | bytes 3678208 | tf_op jit(solution)/shard_map/nhwc,kc->nhwk/dot_general | solution.py:45
  118.1 1.5 collective-permute-start
  121.3 6.8 %collective-permute-done = f32[1,15,15,256]{3,2,1,0:T(8,128)S(1)} collective-permute-done((f32[1,15,15,256]{3,2,1,0:T(8,128)S(1)}, f32[1,15,15,256]{3,2,1,0:T(8,128)S(1)}, u32[]{:S(2)}, u32[]{:S(2)}) %collective-permute-start) | collective-permute-done | bytes 230432 | tf_op jit(solution)/shard_map/ppermute | solution.py:17
  129.6 1.9 reshape.83
  131.4 2.8 convolution_bitcast_fusion.1
  135.2 5.2 %convolution_multiply_fusion = f32[1792,256]{0,1:T(8,128)S(1)} fusion(f32[450,1792]{1,0:T(8,128)} %constant_dynamic-update-slice_fusion.7, f32[450,256]{1,0:T(8,128)S(1)} %copy-done.15), kind=kOutput, calls=%fused_computation.25 | convolution fusion | flops 2477719552 | bytes 5521408 | tf_op jit(solution)/shard_map/rk,rc->kc/dot_general | solution.py:54
  140.4 5.3 %convolution_multiply_fusion.1 = f32[1792,256]{0,1:T(8,128)S(1)} fusion(f32[450,1792]{1,0:T(8,128)} %constant_dynamic-update-slice_fusion, f32[450,256]{1,0:T(8,128)S(1)} %reshape.82), kind=kOutput, calls=%fused_computation.26 | convolution fusion | flops 2477719552 | bytes 5521408 | tf_op jit(solution)/shard_map/rk,rc->kc/dot_general | solution.py:54
  145.7 2.1 pad_maximum_fusion
  147.8 5.2 %copy.58 = f32[1792,512]{1,0:T(8,128)} copy(f32[1792,512]{0,1:T(8,128)} %pad_maximum_fusion) | data formatting | bytes 7340032
  153.2 1.3 copy-done
  154.4 2.6 convolution_bitcast_fusion
  157.3 1.2 copy.55
  158.6 126.1 %reduce-scatter.4.cloned.1.call-done = f32[56,512]{1,0:T(8,128)} async-done(((f32[1792,512]{1,0:T(8,128)}), f32[56,512]{1,0:T(8,128)}) %reduce-scatter.4.cloned.1.call-update) | async-done | bytes 114704
  (102 shorter events, 32.3 us)
Async XLA Ops:
  7.2 13.1 %copy-start.17 = (f32[1,2,1,15,15,256]{5,2,4,3,1,0:T(1,128)S(1)}, f32[1,2,1,15,15,256]{5,2,4,3,1,0:T(1,128)}, u32[]{:S(2)}) copy-start(f32[1,2,1,15,15,256]{5,2,4,3,1,0:T(1,128)} %param.8) | copy-start | bytes 1382404
  9.4 55.9 %all-to-all-start = ((f32[32,56,256]{2,1,0:T(8,128)}), f32[32,56,256]{2,1,0:T(8,128)S(1)}, u32[]{:S(2)}, u32[]{:S(2)}) async-start(f32[32,56,256]{2,1,0:T(8,128)} %stack.27), calls=%async_computation | async-start | bytes 3670016 | tf_op jit(solution)/shard_map/all_to_all | solution.py:10
  19.4 95.0 %all-gather.3.cloned.1.call-start = ((), (), s32[]{:S(2)}) async-start(), calls=%async_computation.2 | async-start | bytes 1892352 | tf_op jit(solution)/shard_map/all_gather | solution.py:62
  20.2 264.5 %reduce-scatter.4.cloned.1.call-start = ((), (), s32[]{:S(2)}) async-start(), calls=%async_computation.3 | async-start | bytes 3784704
  32.4 6.6 %copy-start.20 = (f32[1,1,15,15,256]{4,1,3,2,0:T(1,128)S(1)}, f32[1,1,15,15,256]{4,1,3,2,0:T(1,128)}, u32[]{:S(2)}) copy-start(f32[1,1,15,15,256]{4,1,3,2,0:T(1,128)} %param.10) | copy-start | bytes 691204
  33.2 6.5 %copy-start.16 = (f32[1,2,1,15,15,256]{5,1,4,3,2,0:T(2,128)S(1)}, f32[1,2,1,15,15,256]{5,1,4,3,2,0:T(2,128)}, u32[]{:S(2)}) copy-start(f32[1,2,1,15,15,256]{5,1,4,3,2,0:T(2,128)} %copy.90) | copy-start | bytes 1382404
  41.6 5.6 %copy-start.18 = (f32[2,15,15,256]{3,0,2,1:T(2,128)S(1)}, f32[2,15,15,256]{3,0,2,1:T(2,128)}, u32[]{:S(2)}) copy-start(f32[2,15,15,256]{3,0,2,1:T(2,128)} %get-tuple-element.15) | copy-start | bytes 1382404
  46.3 5.6 %copy-start.4 = (f32[450,256]{1,0:T(8,128)S(1)}, f32[450,256]{1,0:T(8,128)}, u32[]{:S(2)}) copy-start(f32[450,256]{1,0:T(8,128)} %concatenate.47) | copy-start | bytes 1382404
  47.2 7.5 %copy-start.5 = (f32[450,256]{1,0:T(8,128)S(1)}, f32[450,256]{1,0:T(8,128)}, u32[]{:S(2)}) copy-start(f32[450,256]{1,0:T(8,128)} %concatenate.48) | copy-start | bytes 1382404
  52.0 5.5 %copy-start.6 = (f32[450,256]{1,0:T(8,128)S(1)}, f32[450,256]{1,0:T(8,128)}, u32[]{:S(2)}) copy-start(f32[450,256]{1,0:T(8,128)} %concatenate.50) | copy-start | bytes 1382404
  52.0 6.3 %copy-start.7 = (f32[450,256]{1,0:T(8,128)S(1)}, f32[450,256]{1,0:T(8,128)}, u32[]{:S(2)}) copy-start(f32[450,256]{1,0:T(8,128)} %concatenate.51) | copy-start | bytes 1382404
  52.0 7.2 %copy-start.9 = (f32[450,256]{1,0:T(8,128)S(1)}, f32[450,256]{1,0:T(8,128)}, u32[]{:S(2)}) copy-start(f32[450,256]{1,0:T(8,128)} %concatenate.52) | copy-start | bytes 1382404
  52.0 8.0 %copy-start.10 = (f32[450,256]{1,0:T(8,128)S(1)}, f32[450,256]{1,0:T(8,128)}, u32[]{:S(2)}) copy-start(f32[450,256]{1,0:T(8,128)} %concatenate.53) | copy-start | bytes 1382404
  52.8 8.0 %copy-start.11 = (f32[450,256]{1,0:T(8,128)S(1)}, f32[450,256]{1,0:T(8,128)}, u32[]{:S(2)}) copy-start(f32[450,256]{1,0:T(8,128)} %concatenate.40) | copy-start | bytes 1382404
  54.7 7.0 %copy-start.13 = (f32[450,256]{1,0:T(8,128)S(1)}, f32[450,256]{1,0:T(8,128)}, u32[]{:S(2)}) copy-start(f32[450,256]{1,0:T(8,128)} %concatenate.41) | copy-start | bytes 1382404
  55.5 7.0 %copy-start.12 = (f32[450,256]{1,0:T(8,128)S(1)}, f32[450,256]{1,0:T(8,128)}, u32[]{:S(2)}) copy-start(f32[450,256]{1,0:T(8,128)} %concatenate.42) | copy-start | bytes 1382404
  57.4 6.0 %copy-start.14 = (f32[450,256]{1,0:T(8,128)S(1)}, f32[450,256]{1,0:T(8,128)}, u32[]{:S(2)}) copy-start(f32[450,256]{1,0:T(8,128)} %concatenate.43) | copy-start | bytes 1382404
  58.3 6.0 %copy-start.24 = (s32[1,2,1,15,15,256]{5,2,4,3,1,0:T(1,128)S(1)}, s32[1,2,1,15,15,256]{5,2,4,3,1,0:T(1,128)}, u32[]{:S(2)}) copy-start(s32[1,2,1,15,15,256]{5,2,4,3,1,0:T(1,128)} %param.9) | copy-start | bytes 1382404
  114.5 5.1 %copy-start.3 = (f32[450,256]{1,0:T(8,128)S(1)}, f32[450,256]{1,0:T(8,128)}, u32[]{:S(2)}) copy-start(f32[450,256]{1,0:T(8,128)} %concatenate.44) | copy-start | bytes 1382404
  114.5 5.9 %copy-start.8 = (f32[450,256]{1,0:T(8,128)S(1)}, f32[450,256]{1,0:T(8,128)}, u32[]{:S(2)}) copy-start(f32[450,256]{1,0:T(8,128)} %concatenate.45) | copy-start | bytes 1382404
  114.5 13.6 %copy-start.19 = (f32[1,1,15,15,256]{4,1,3,2,0:T(1,128)S(1)}, f32[1,1,15,15,256]{4,1,3,2,0:T(1,128)}, u32[]{:S(2)}) copy-start(f32[1,1,15,15,256]{4,1,3,2,0:T(1,128)} %param.11) | copy-start | bytes 691204
  117.9 10.9 %copy-start.22 = (f32[1,1,15,15,256]{4,3,2,1,0:T(8,128)S(1)}, f32[1,1,15,15,256]{4,3,2,1,0:T(8,128)}, u32[]{:S(2)}) copy-start(f32[1,1,15,15,256]{4,3,2,1,0:T(8,128)} %copy.54) | copy-start | bytes 691204
  118.1 10.0 %collective-permute-start = (f32[1,15,15,256]{3,2,1,0:T(8,128)S(1)}, f32[1,15,15,256]{3,2,1,0:T(8,128)S(1)}, u32[]{:S(2)}, u32[]{:S(2)}) collective-permute-start(f32[1,15,15,256]{3,2,1,0:T(8,128)S(1)} %fusion.21), channel_id=1, source_target_pairs={{32,0},{64,32},{96,64},{128,96},{160,128},{192,160},{224,192},{256... | collective-permute-start | bytes 691208 | tf_op jit(solution)/shard_map/ppermute | solution.py:17
  128.0 0.7 copy-start.21
  131.4 2.8 copy-start.23
  131.4 3.6 %copy-start.1 = (f32[1,15,15,256]{3,2,1,0:T(8,128)S(1)}, f32[1,15,15,256]{3,2,1,0:T(8,128)}, u32[]{:S(2)}) copy-start(f32[1,15,15,256]{3,2,1,0:T(8,128)} %fusion.8) | copy-start | bytes 691204
  134.2 1.0 copy-start.15
  134.4 0.7 copy-start.2
  152.9 1.5 copy-start
Sparse Core Ops, SparseCore 0:
  23.6 90.8 all-gather.2
  153.1 131.5 reduce-scatter.3
